TPU v7x, 256 devices: a whole 4x4x8 slice. The times are simulated.
256 devices in a mesh: wide: 32 (over z, x_lo, core), tm: 8 (over x_hi, y).
Axes of the slice: x: 4 (x_hi: 2, x_lo: 2; x = x_hi * 2 + x_lo), y: 4, z: 8, core: 2. Of those that a mesh axis runs over, the one named last changes fastest.
Arguments:
- clips_in: bfloat16 [32, 32, 14, 14, 256], P('wide', 'tm'), may hold values from -6 to 6
- w_spatial: bfloat16 [3, 3, 256, 256], replicated, may hold values from -0.125 to 0.125
- w_temporal: bfloat16 [3, 256, 256], replicated, may hold values from -0.21875 to 0.21875
- w_proj: bfloat16 [256, 512], replicated, may hold values from -0.375 to 0.375
- prompts: bfloat16 [4096, 512], P('tm'), may hold values from -6 to 6
- positives: int32 [32, 4], P('wide'), may hold values from 0 to 4095
Outputs:
- grad_spatial: float32 [3, 3, 256, 256], replicated
- grad_temporal: float32 [3, 256, 256], replicated
- grad_proj: float32 [256, 512], replicated
- grad_prompts: float32 [4096, 512], P('tm')
Inputs may be any that keep to these rules, and one draw needn't show every extreme that they name: `positives`: 4 positive prompt ids for each clip; a clip may name one id more than once.
All inputs are finite; a program needn't handle non-finite values.
Results may differ from a plain program's by a relative error of at most 0.0037.
Values may be sent and summed in bfloat16 or wider, within the bound.
A program may use at most 64 MiB of HBM per device.

v0:
```python
import jax
import jax.numpy as jnp
from jax import lax
from jax.sharding import PartitionSpec as P

HI = lax.Precision.HIGHEST


def extended(block, sides, width):
    for axis, dim in sides:
        count = lax.axis_size(axis)
        forward = [(i, i + 1) for i in range(count - 1)]
        backward = [(target, source) for source, target in forward]
        low = lax.ppermute(
            lax.slice_in_dim(block, block.shape[dim] - width, None, axis=dim), axis, forward
        )
        high = lax.ppermute(lax.slice_in_dim(block, 0, width, axis=dim), axis, backward)
        block = jnp.concatenate([low, block, high], axis=dim)
    return block


def dsilu(v):
    sig = jax.nn.sigmoid(v)
    return sig * (1.0 + v * (1.0 - sig))


def contract(left, right):
    return lax.dot_general(
        left, right, (((0,), (0,)), ((), ())), preferred_element_type=jnp.float32
    )


def count_hits(pos_ids, ids):
    return jnp.sum((pos_ids[:, :, None] == ids[None, None, :]).astype(jnp.float32), axis=1)


def body(clips_in, w_spatial, w_temporal, w_proj, prompts, positives):
    clips, frames, side, unused, chan = clips_in.shape
    rows = clips * frames * side * side
    padded = jnp.pad(clips_in, ((0, 0), (0, 0), (1, 1), (1, 1), (0, 0)))
    pre_s = jnp.zeros((rows, chan), jnp.float32)
    for a in range(3):
        for b in range(3):
            window = padded[:, :, a : a + side, b : b + side, :].reshape(rows, chan)
            pre_s = pre_s + jnp.dot(window, w_spatial[a, b], preferred_element_type=jnp.float32)
    act = jax.nn.silu(pre_s).astype(jnp.bfloat16).reshape(clips, frames, side, side, chan)
    act_wide = extended(act, (("tm", 1),), 1)
    pre_t = jnp.zeros((rows, chan), jnp.float32)
    for t in range(3):
        pre_t = pre_t + jnp.dot(
            act_wide[:, t : t + frames].reshape(rows, chan),
            w_temporal[t],
            preferred_element_type=jnp.float32,
        )
    out = clips_in.reshape(rows, chan).astype(jnp.float32) + jax.nn.silu(pre_t)
    pooled_loc = jnp.sum(out.reshape(clips, frames * side * side, chan), axis=1)
    pooled = lax.psum(pooled_loc, "tm")
    proj32 = w_proj.astype(jnp.float32)
    z = jnp.dot(pooled, proj32, precision=HI)
    znorm = jnp.sqrt(jnp.sum(z * z, axis=1, keepdims=True) + 1e-06)
    zhat = z / znorm
    p32 = prompts.astype(jnp.float32)
    pnorm = jnp.sqrt(jnp.sum(p32 * p32, axis=1, keepdims=True) + 1e-06)
    phat = p32 / pnorm
    expo = jnp.exp(16.0 * jnp.dot(zhat, phat.T, precision=HI))
    shard = phat.shape[0]
    ids = lax.axis_index("tm") * shard + jnp.arange(shard, dtype=jnp.int32)
    multi = count_hits(positives, ids)
    pos_expo = multi * expo
    total, pos_total = lax.psum(
        (jnp.sum(expo, axis=1, keepdims=True), jnp.sum(pos_expo, axis=1, keepdims=True)), "tm"
    )
    g_s = expo / total - pos_expo / pos_total
    g_zhat = lax.psum(16.0 * jnp.dot(g_s, phat, precision=HI), "tm")
    g_phat = lax.psum(16.0 * jnp.dot(g_s.T, zhat, precision=HI), "wide")
    grad_prompts = (g_phat - phat * jnp.sum(phat * g_phat, axis=1, keepdims=True)) / pnorm
    g_z = (g_zhat - zhat * jnp.sum(zhat * g_zhat, axis=1, keepdims=True)) / znorm
    proj_term = jnp.dot(pooled_loc.T, g_z, precision=HI)
    g_pooled = jnp.dot(g_z, proj32.T, precision=HI)
    g_t = (g_pooled[:, None, :] * dsilu(pre_t).reshape(clips, frames * side * side, chan)).astype(
        jnp.bfloat16
    )
    g_t_flat = g_t.reshape(rows, chan)
    temporal_term = jnp.stack(
        [contract(act_wide[:, t : t + frames].reshape(rows, chan), g_t_flat) for t in range(3)]
    )
    g_wide = extended(g_t.reshape(clips, frames, side, side, chan), (("tm", 1),), 1)
    g_act = jnp.zeros((rows, chan), jnp.float32)
    for t in range(3):
        g_act = g_act + jnp.dot(
            g_wide[:, 2 - t : 2 - t + frames].reshape(rows, chan),
            w_temporal[t].T,
            preferred_element_type=jnp.float32,
        )
    g_sp = (g_act * dsilu(pre_s)).astype(jnp.bfloat16)
    spatial_term = jnp.stack(
        [
            jnp.stack(
                [
                    contract(padded[:, :, a : a + side, b : b + side, :].reshape(rows, chan), g_sp)
                    for b in range(3)
                ]
            )
            for a in range(3)
        ]
    )
    spatial_sum, temporal_sum, proj_sum = lax.psum(
        (spatial_term, temporal_term, proj_term), ("wide", "tm")
    )
    return (spatial_sum, temporal_sum, proj_sum, grad_prompts)


def solution(mesh):
    placed = (P("wide", "tm", None, None, None), P(), P(), P(), P("tm", None), P("wide", None))
    return jax.shard_map(
        body, mesh=mesh, in_specs=placed, out_specs=(P(), P(), P(), P("tm", None)), check_vma=False
    )
```

profile of v0, /device:TPU:8, one launch (start us, length us, event | category | flops | bytes accessed | tf_op | source)
XLA Modules:
  0.0 645.8 jit_solution(18042460652931843559)
XLA Ops:
  8.3 3.9 pad_slice_fusion.1
  19.8 1.3 fusion.23
  26.0 3.5 collective-permute-start
  29.5 2.4 collective-permute-start.1
  32.1 2.1 fusion.11
  34.3 2.1 collective-permute-done.1
  38.3 1.3 fusion.7
  39.6 2.2 add_reduce_fusion
  41.9 20.6 %psum.56 = f32[256]{0:T(256)S(1)} all-reduce(f32[256]{0:T(256)S(1)} %get-tuple-element.29), channel_id=1, replica_groups=mesh['wide'=32,'tm'=8] {'tm'}, use_global_device_ids=true, to_apply=%region_1.2 | all-reduce | flops 256 | bytes 2048 | tf_op jit(solution)/shard_map/psum | solution.py:57
  65.7 22.4 %all-reduce.2 = (f32[]{:T(128)}, f32[]{:T(128)}) all-reduce(f32[]{:T(128)} %get-tuple-element.5, f32[]{:T(128)} %get-tuple-element.4), channel_id=1, replica_groups=mesh['wide'=32,'tm'=8] {'tm'}, use_global_device_ids=true, to_apply=%region_8.9 | all-reduce | flops 2 | bytes 16 | tf_op jit(solution)/shard_map/psum | solution.py:70
  88.1 1.3 divide_subtract_fusion
  90.2 19.0 %psum.59 = f32[1,512]{1,0:T(1,128)S(1)} all-reduce(f32[1,512]{1,0:T(1,128)S(1)} %bitcast.147), channel_id=1, replica_groups=mesh['wide'=32,'tm'=8] {'tm'}, use_global_device_ids=true, to_apply=%region_9.10 | all-reduce | flops 512 | bytes 4096 | tf_op jit(solution)/shard_map/psum | solution.py:74
  110.8 1.4 multiply_convert_fusion
  114.8 2.1 fusion.9
  118.1 7.1 %collective-permute-start.2 = (bf16[1,1,14,14,256]{4,3,2,1,0:T(8,128)(2,1)S(1)}, bf16[1,1,14,14,256]{4,3,2,1,0:T(8,128)(2,1)S(1)}, u32[]{:S(2)}, u32[]{:S(2)}) collective-permute-start(bf16[1,1,14,14,256]{4,3,2,1,0:T(8,128)(2,1)S(1)} %get-tuple-element.13), channel_id=1, source_target_pairs={{1,0},{2,1},{3,2},{4,3},{5,4},{6,5},{7,6},{9,8},{10,9},{11,10},{12... | collective-permute-start | bytes 301064 | tf_op jit(solution)/shard_map/ppermute | solution.py:17
  125.2 1.9 collective-permute-start.3
  129.2 2.6 collective-permute-done.3
  133.0 1.3 fusion.5
  134.5 1.5 fusion.3
  140.6 1.6 pad_maximum_fusion
  142.2 215.7 %all-reduce.6.cloned.1.call-done = f32[512,512]{1,0:T(8,128)} async-done(((f32[512,512]{1,0:T(8,128)}), f32[512,512]{1,0:T(8,128)}) %all-reduce.6.cloned.1.call-update) | async-done | bytes 1048592 | tf_op jit(solution)/shard_map/psum | solution.py:75
  357.9 1.6 multiply_reduce_fusion
  360.7 272.8 %all-reduce.8.cloned.1.call-done = (f32[3,3,256,256]{3,2,1,0:T(8,128)}, f32[3,256,256]{2,1,0:T(8,128)}, f32[256,512]{1,0:T(8,128)}) async-done(((f32[3,3,256,256]{3,2,1,0:T(8,128)}, f32[3,256,256]{2,1,0:T(8,128)}, f32[256,512]{1,0:T(8,128)}), (f32[3,3,256,256]{3,2,1,0:T(8,128)}, f32[3,256,256]{2,1,0:T(8,128)}, f32[256,512]{1,0:T(8,128)})) %all-reduce.8.cloned.1.call-update) | async-done | bytes 3670032 | tf_op jit(solution)/shard_map/psum | solution.py:107
  633.5 3.3 copy.37
  (135 shorter events, 35.3 us)
Async XLA Ops:
  7.2 55.3 %copy-start = (bf16[256,512]{1,0:T(8,128)(2,1)S(1)}, bf16[256,512]{1,0:T(8,128)(2,1)}, u32[]{:S(2)}) copy-start(bf16[256,512]{1,0:T(8,128)(2,1)} %param.9) | copy-start | bytes 786436
  7.2 350.7 %all-reduce.6.cloned.1.call-start = ((), (), s32[]{:S(2)}) async-start(), calls=%async_computation | async-start | bytes 2097152 | tf_op jit(solution)/shard_map/psum | solution.py:75
  13.6 10.1 %copy-start.5 = (bf16[784,256]{1,0:T(8,128)(2,1)}, bf16[784,256]{1,0:T(8,128)(2,1)S(1)}, u32[]{:S(2)}) copy-start(bf16[784,256]{1,0:T(8,128)(2,1)S(1)} %reshape.210) | copy-start | bytes 1204228
  14.0 7.6 %copy-start.3 = (bf16[784,256]{1,0:T(8,128)(2,1)}, bf16[784,256]{1,0:T(8,128)(2,1)S(1)}, u32[]{:S(2)}) copy-start(bf16[784,256]{1,0:T(8,128)(2,1)S(1)} %reshape.206) | copy-start | bytes 1204228
  14.2 7.6 %copy-start.7 = (bf16[784,256]{1,0:T(8,128)(2,1)}, bf16[784,256]{1,0:T(8,128)(2,1)S(1)}, u32[]{:S(2)}) copy-start(bf16[784,256]{1,0:T(8,128)(2,1)S(1)} %reshape.207) | copy-start | bytes 1204228
  15.5 6.8 %copy-start.9 = (bf16[784,256]{1,0:T(8,128)(2,1)}, bf16[784,256]{1,0:T(8,128)(2,1)S(1)}, u32[]{:S(2)}) copy-start(bf16[784,256]{1,0:T(8,128)(2,1)S(1)} %reshape.208) | copy-start | bytes 1204228
  19.8 1.8 copy-start.13
  19.8 1.5 copy-start.15
  25.9 6.0 copy-start.1
  26.0 8.2 %copy-start.27 = (s32[1,4]{1,0:T(1,128)S(1)}, s32[1,4]{1,0:T(1,128)}, u32[]{:S(2)}) copy-start(s32[1,4]{1,0:T(1,128)} %param.11) | copy-start | bytes 52
  26.0 8.2 %collective-permute-start = (bf16[1,1,14,14,256]{4,3,2,1,0:T(8,128)(2,1)S(1)}, bf16[1,1,14,14,256]{4,3,2,1,0:T(8,128)(2,1)S(1)}, u32[]{:S(2)}, u32[]{:S(2)}) collective-permute-start(bf16[1,1,14,14,256]{4,3,2,1,0:T(8,128)(2,1)S(1)} %get-tuple-element.17), channel_id=1, source_target_pairs={{0,1},{1,2},{2,3},{3,4},{4,5},{5,6},{6,7},{8,9},{9,10},{10,11},{11... | collective-permute-start | bytes 301064 | tf_op jit(solution)/shard_map/ppermute | solution.py:14
  29.5 6.8 %collective-permute-start.1 = (bf16[1,1,14,14,256]{4,3,2,1,0:T(8,128)(2,1)S(1)}, bf16[1,1,14,14,256]{4,3,2,1,0:T(8,128)(2,1)}, u32[]{:S(2)}, u32[]{:S(2)}) collective-permute-start(bf16[1,1,14,14,256]{4,3,2,1,0:T(8,128)(2,1)S(1)} %get-tuple-element.18), channel_id=1, source_target_pairs={{1,0},{2,1},{3,2},{4,3},{5,4},{6,5},{7,6},{9,8},{10,9},{11,10},{12... | collective-permute-start | bytes 301064 | tf_op jit(solution)/shard_map/ppermute | solution.py:17
  112.2 2.1 copy-start.23
  118.0 10.3 %copy-start.25 = (f32[1,256,256]{2,1,0:T(8,128)S(1)}, f32[1,256,256]{2,1,0:T(8,128)}, u32[]{:S(2)}) copy-start(f32[1,256,256]{2,1,0:T(8,128)} %convolution_bitcast_fusion) | copy-start | bytes 786436
  118.0 10.3 %copy-start.26 = (f32[1,256,256]{2,1,0:T(8,128)S(1)}, f32[1,256,256]{2,1,0:T(8,128)}, u32[]{:S(2)}) copy-start(f32[1,256,256]{2,1,0:T(8,128)} %convolution_bitcast_fusion.1) | copy-start | bytes 786436
  118.1 11.2 %collective-permute-start.2 = (bf16[1,1,14,14,256]{4,3,2,1,0:T(8,128)(2,1)S(1)}, bf16[1,1,14,14,256]{4,3,2,1,0:T(8,128)(2,1)S(1)}, u32[]{:S(2)}, u32[]{:S(2)}) collective-permute-start(bf16[1,1,14,14,256]{4,3,2,1,0:T(8,128)(2,1)S(1)} %get-tuple-element.13), channel_id=1, source_target_pairs={{1,0},{2,1},{3,2},{4,3},{5,4},{6,5},{7,6},{9,8},{10,9},{11,10},{12... | collective-permute-start | bytes 301064 | tf_op jit(solution)/shard_map/ppermute | solution.py:17
  125.2 6.7 %collective-permute-start.3 = (bf16[1,1,14,14,256]{4,3,2,1,0:T(8,128)(2,1)S(1)}, bf16[1,1,14,14,256]{4,3,2,1,0:T(8,128)(2,1)S(1)}, u32[]{:S(2)}, u32[]{:S(2)}) collective-permute-start(bf16[1,1,14,14,256]{4,3,2,1,0:T(8,128)(2,1)S(1)} %get-tuple-element.14), channel_id=1, source_target_pairs={{0,1},{1,2},{2,3},{3,4},{4,5},{5,6},{6,7},{8,9},{9,10},{10,11},{11... | collective-permute-start | bytes 301064 | tf_op jit(solution)/shard_map/ppermute | solution.py:14
  128.1 505.5 %all-reduce.8.cloned.1.call-start = ((), (), s32[]{:S(2)}) async-start(), calls=%async_computation.1 | async-start | bytes 7340032 | tf_op jit(solution)/shard_map/psum | solution.py:107
  132.9 1.5 copy-start.16
  133.0 1.5 copy-start.28
  134.5 1.5 copy-start.21
  134.5 1.9 copy-start.6
  357.9 1.6 copy-start.2
  633.5 3.3 copy-start.18
  (11 other events, 12.3 us)
Sparse Core Ops, SparseCore 0:
  128.2 229.6 all-reduce.5
  365.2 268.2 all-reduce.7
where the time goes:
time: 647 us; the launch traced here: 646 us
  waiting for transfers between devices  493 us (76%)
  blocking collectives  62 us (10%)
  local copies, waits for them, and re-layouts  23.1 us (4%)
  matrix products  22.6 us (3%)
  between operations  15.4 us (2%)
  starting transfers between devices  15.2 us (2%)
  other arithmetic  14.3 us (2%)
    psum x1, waiting for transfers between devices, body(): lax.psum((spatial_term, temporal_term, proj_term), ('wide', 'tm'))  273 us
    psum x1, waiting for transfers between devices, body(): g_phat = lax.psum(16.0 * jnp.dot(g_s.T, zhat, precision=HI), 'wide')  216 us
    psum x1, blocking collectives, body(): lax.psum((jnp.sum(expo, axis=1, keepdims=True), jnp.sum(pos_expo, axis=1,...  22.4 us
    psum x1, blocking collectives, body(): pooled = lax.psum(pooled_loc, 'tm')  20.6 us
    psum x1, blocking collectives, body(): g_zhat = lax.psum(16.0 * jnp.dot(g_s, phat, precision=HI), 'tm')  19 us
  transfers between devices with their start and end apart: 6, of which 4 were waited for; matrix products, arithmetic and copies ran while one was open for 2% of the time, Pallas kernels for 0%

commit v1 on v0

--- a/solution.py
+++ b/solution.py
@@ -105,7 +105,7 @@
         ]
     )
     spatial_sum, temporal_sum, proj_sum = lax.psum(
-        (spatial_term, temporal_term, proj_term), ("wide", "tm")
+        lax.psum((spatial_term, temporal_term, proj_term), "tm"), "wide"
     )
     return (spatial_sum, temporal_sum, proj_sum, grad_prompts)
 

time: 647 us -> 515 us (0.80)
  waiting for transfers between devices: 493 us -> 362 us
    psum x2, waiting for transfers between devices: 488 us -> 357 us  [the longest x1 246 us: body(): lax.psum(lax.psum((spatial_term, temporal_term, proj_term), 'tm'), 'wide')]
  transfers between devices with their start and end apart: 6 -> 6, of which waited for: 4 -> 4; matrix products, arithmetic and copies ran while one was open for 2% -> 1% of each run, Pallas kernels for 0% -> 0%
where the time goes in v1:
time: 515 us; the launch traced here: 514 us
  waiting for transfers between devices  362 us (70%)
  blocking collectives  62 us (12%)
  local copies, waits for them, and re-layouts  22.9 us (4%)
  matrix products  22.8 us (4%)
  between operations  15.4 us (3%)
  starting transfers between devices  15.1 us (3%)
  other arithmetic  14.3 us (3%)
    psum x1, waiting for transfers between devices, body(): lax.psum(lax.psum((spatial_term, temporal_term, proj_term), 'tm'), 'wide')  246 us
    psum x1, waiting for transfers between devices, body(): lax.psum((spatial_term, temporal_term, proj_term), 'tm')  111 us
    psum x1, blocking collectives, body(): lax.psum((jnp.sum(expo, axis=1, keepdims=True), jnp.sum(pos_expo, axis=1,...  22.4 us
    psum x1, blocking collectives, body(): pooled = lax.psum(pooled_loc, 'tm')  20.6 us
    psum x1, blocking collectives, body(): g_zhat = lax.psum(16.0 * jnp.dot(g_s, phat, precision=HI), 'tm')  19 us
  transfers between devices with their start and end apart: 6, of which 4 were waited for; matrix products, arithmetic and copies ran while one was open for 1% of the time, Pallas kernels for 0%

profile of v1, /device:TPU:8, one launch (start us, length us, event | category | flops | bytes accessed | tf_op | source)
XLA Modules:
  0.0 514.1 jit_solution(8214170956434532699)
XLA Ops:
  8.3 4.3 pad_slice_fusion.1
  20.8 1.4 fusion.23
  27.0 3.5 collective-permute-start
  30.5 2.3 collective-permute-start.1
  33.1 2.1 fusion.11
  35.3 2.1 collective-permute-done.1
  39.4 1.3 fusion.7
  40.7 2.2 add_reduce_fusion
  42.9 20.6 %psum.77 = f32[256]{0:T(256)S(1)} all-reduce(f32[256]{0:T(256)S(1)} %get-tuple-element.33), channel_id=1, replica_groups=mesh['wide'=32,'tm'=8] {'tm'}, use_global_device_ids=true, to_apply=%region_1.2 | all-reduce | flops 256 | bytes 2048 | tf_op jit(solution)/shard_map/psum | solution.py:57
  66.8 22.4 %all-reduce.2 = (f32[]{:T(128)}, f32[]{:T(128)}) all-reduce(f32[]{:T(128)} %get-tuple-element.5, f32[]{:T(128)} %get-tuple-element.4), channel_id=1, replica_groups=mesh['wide'=32,'tm'=8] {'tm'}, use_global_device_ids=true, to_apply=%region_8.9 | all-reduce | flops 2 | bytes 16 | tf_op jit(solution)/shard_map/psum | solution.py:70
  89.2 1.3 divide_subtract_fusion
  91.3 19.0 %psum.80 = f32[1,512]{1,0:T(1,128)S(1)} all-reduce(f32[1,512]{1,0:T(1,128)S(1)} %bitcast.147), channel_id=1, replica_groups=mesh['wide'=32,'tm'=8] {'tm'}, use_global_device_ids=true, to_apply=%region_9.10 | all-reduce | flops 512 | bytes 4096 | tf_op jit(solution)/shard_map/psum | solution.py:74
  111.8 1.4 multiply_convert_fusion
  115.9 2.1 fusion.9
  118.1 7.0 %collective-permute-start.2 = (bf16[1,1,14,14,256]{4,3,2,1,0:T(8,128)(2,1)S(1)}, bf16[1,1,14,14,256]{4,3,2,1,0:T(8,128)(2,1)S(1)}, u32[]{:S(2)}, u32[]{:S(2)}) collective-permute-start(bf16[1,1,14,14,256]{4,3,2,1,0:T(8,128)(2,1)S(1)} %get-tuple-element.17), channel_id=1, source_target_pairs={{1,0},{2,1},{3,2},{4,3},{5,4},{6,5},{7,6},{9,8},{10,9},{11,10},{12... | collective-permute-start | bytes 301064 | tf_op jit(solution)/shard_map/ppermute | solution.py:17
  125.1 2.1 collective-permute-start.3
  129.0 2.7 collective-permute-done.3
  132.9 1.3 fusion.5
  134.4 1.5 fusion.3
  140.2 1.6 pad_maximum_fusion
  142.9 110.6 %all-reduce.9.cloned.1.call-done = (f32[3,3,256,256]{3,2,1,0:T(8,128)}, f32[3,256,256]{2,1,0:T(8,128)}, f32[256,512]{1,0:T(8,128)}) async-done(((f32[3,3,256,256]{3,2,1,0:T(8,128)}, f32[3,256,256]{2,1,0:T(8,128)}, f32[256,512]{1,0:T(8,128)}), (f32[3,3,256,256]{3,2,1,0:T(8,128)}, f32[3,256,256]{2,1,0:T(8,128)}, f32[256,512]{1,0:T(8,128)})) %all-reduce.9.cloned.1.call-update) | async-done | bytes 3670032 | tf_op jit(solution)/shard_map/psum | solution.py:108
  253.5 246.3 %all-reduce.7.cloned.1.call-done = (f32[3,3,256,256]{3,2,1,0:T(8,128)}, f32[3,256,256]{2,1,0:T(8,128)}, f32[256,512]{1,0:T(8,128)}, f32[512,512]{1,0:T(8,128)}) async-done(((f32[3,3,256,256]{3,2,1,0:T(8,128)}, f32[3,256,256]{2,1,0:T(8,128)}, f32[256,512]{1,0:T(8,128)}, f32[512,512]{1,0:T(8,128)}), (f32[3,3,256,256]{3,2,1,0:T(8,128)}, f32[3,256,256]{2,1,0:T(8,128)}, f32[256,512]{1,0:T(8,128)}, ...) | async-done | bytes 4718608 | tf_op jit(solution)/shard_map/psum | solution.py:107
  499.8 1.6 multiply_reduce_fusion
  503.5 1.4 copy.40
  (135 shorter events, 36.6 us)
Async XLA Ops:
  7.2 56.3 %copy-start = (bf16[256,512]{1,0:T(8,128)(2,1)S(1)}, bf16[256,512]{1,0:T(8,128)(2,1)}, u32[]{:S(2)}) copy-start(bf16[256,512]{1,0:T(8,128)(2,1)} %param.9) | copy-start | bytes 786436
  7.2 246.3 %all-reduce.9.cloned.1.call-start = ((), (), s32[]{:S(2)}) async-start(), calls=%async_computation.1 | async-start | bytes 7340032 | tf_op jit(solution)/shard_map/psum | solution.py:108
  12.9 11.8 %copy-start.6 = (bf16[784,256]{1,0:T(8,128)(2,1)}, bf16[784,256]{1,0:T(8,128)(2,1)S(1)}, u32[]{:S(2)}) copy-start(bf16[784,256]{1,0:T(8,128)(2,1)S(1)} %reshape.210) | copy-start | bytes 1204228
  13.3 9.3 %copy-start.4 = (bf16[784,256]{1,0:T(8,128)(2,1)}, bf16[784,256]{1,0:T(8,128)(2,1)S(1)}, u32[]{:S(2)}) copy-start(bf16[784,256]{1,0:T(8,128)(2,1)S(1)} %reshape.206) | copy-start | bytes 1204228
  13.5 9.3 %copy-start.8 = (bf16[784,256]{1,0:T(8,128)(2,1)}, bf16[784,256]{1,0:T(8,128)(2,1)S(1)}, u32[]{:S(2)}) copy-start(bf16[784,256]{1,0:T(8,128)(2,1)S(1)} %reshape.207) | copy-start | bytes 1204228
  14.9 8.5 %copy-start.10 = (bf16[784,256]{1,0:T(8,128)(2,1)}, bf16[784,256]{1,0:T(8,128)(2,1)S(1)}, u32[]{:S(2)}) copy-start(bf16[784,256]{1,0:T(8,128)(2,1)S(1)} %reshape.208) | copy-start | bytes 1204228
  20.8 1.5 copy-start.15
  26.9 6.0 %copy-start.1 = (bf16[512,512]{1,0:T(8,128)(2,1)S(1)}, bf16[512,512]{1,0:T(8,128)(2,1)}, u32[]{:S(2)}) copy-start(bf16[512,512]{1,0:T(8,128)(2,1)} %param.10) | copy-start | bytes 1572868
  27.0 8.2 %copy-start.27 = (s32[1,4]{1,0:T(1,128)S(1)}, s32[1,4]{1,0:T(1,128)}, u32[]{:S(2)}) copy-start(s32[1,4]{1,0:T(1,128)} %param.11) | copy-start | bytes 52
  27.0 8.2 %collective-permute-start = (bf16[1,1,14,14,256]{4,3,2,1,0:T(8,128)(2,1)S(1)}, bf16[1,1,14,14,256]{4,3,2,1,0:T(8,128)(2,1)S(1)}, u32[]{:S(2)}, u32[]{:S(2)}) collective-permute-start(bf16[1,1,14,14,256]{4,3,2,1,0:T(8,128)(2,1)S(1)} %get-tuple-element.21), channel_id=1, source_target_pairs={{0,1},{1,2},{2,3},{3,4},{4,5},{5,6},{6,7},{8,9},{9,10},{10,11},{11... | collective-permute-start | bytes 301064 | tf_op jit(solution)/shard_map/ppermute | solution.py:14
  30.5 6.8 %collective-permute-start.1 = (bf16[1,1,14,14,256]{4,3,2,1,0:T(8,128)(2,1)S(1)}, bf16[1,1,14,14,256]{4,3,2,1,0:T(8,128)(2,1)}, u32[]{:S(2)}, u32[]{:S(2)}) collective-permute-start(bf16[1,1,14,14,256]{4,3,2,1,0:T(8,128)(2,1)S(1)} %get-tuple-element.22), channel_id=1, source_target_pairs={{1,0},{2,1},{3,2},{4,3},{5,4},{6,5},{7,6},{9,8},{10,9},{11,10},{12... | collective-permute-start | bytes 301064 | tf_op jit(solution)/shard_map/ppermute | solution.py:17
  113.3 2.1 copy-start.23
  115.9 12.2 %copy-start.25 = (f32[1,256,256]{2,1,0:T(8,128)S(1)}, f32[1,256,256]{2,1,0:T(8,128)}, u32[]{:S(2)}) copy-start(f32[1,256,256]{2,1,0:T(8,128)} %convolution_bitcast_fusion) | copy-start | bytes 786436
  115.9 12.2 %copy-start.26 = (f32[1,256,256]{2,1,0:T(8,128)S(1)}, f32[1,256,256]{2,1,0:T(8,128)}, u32[]{:S(2)}) copy-start(f32[1,256,256]{2,1,0:T(8,128)} %convolution_bitcast_fusion.1) | copy-start | bytes 786436
  118.1 11.0 %collective-permute-start.2 = (bf16[1,1,14,14,256]{4,3,2,1,0:T(8,128)(2,1)S(1)}, bf16[1,1,14,14,256]{4,3,2,1,0:T(8,128)(2,1)S(1)}, u32[]{:S(2)}, u32[]{:S(2)}) collective-permute-start(bf16[1,1,14,14,256]{4,3,2,1,0:T(8,128)(2,1)S(1)} %get-tuple-element.17), channel_id=1, source_target_pairs={{1,0},{2,1},{3,2},{4,3},{5,4},{6,5},{7,6},{9,8},{10,9},{11,10},{12... | collective-permute-start | bytes 301064 | tf_op jit(solution)/shard_map/ppermute | solution.py:17
  125.1 6.7 %collective-permute-start.3 = (bf16[1,1,14,14,256]{4,3,2,1,0:T(8,128)(2,1)S(1)}, bf16[1,1,14,14,256]{4,3,2,1,0:T(8,128)(2,1)S(1)}, u32[]{:S(2)}, u32[]{:S(2)}) collective-permute-start(bf16[1,1,14,14,256]{4,3,2,1,0:T(8,128)(2,1)S(1)} %get-tuple-element.18), channel_id=1, source_target_pairs={{0,1},{1,2},{2,3},{3,4},{4,5},{5,6},{6,7},{8,9},{9,10},{10,11},{11... | collective-permute-start | bytes 301064 | tf_op jit(solution)/shard_map/ppermute | solution.py:14
  132.8 1.5 copy-start.16
  132.9 1.5 copy-start.28
  134.4 1.5 copy-start.21
  134.4 1.9 copy-start.7
  141.8 358.0 %all-reduce.7.cloned.1.call-start = ((), (), s32[]{:S(2)}) async-start(), calls=%async_computation | async-start | bytes 9437184 | tf_op jit(solution)/shard_map/psum | solution.py:107
  499.8 1.6 copy-start.2
  501.4 2.0 copy-start.3
  503.5 1.7 copy-start.18
  (11 other events, 12.3 us)
Sparse Core Ops, SparseCore 0:
  141.9 111.5 all-reduce.8
  256.9 242.8 all-reduce.6
